TPU v7x, 256 devices: a whole 4x4x8 slice. The times are simulated.
256 devices in a mesh: row: 8 (over x, core), col: 32 (over y, z).
Axes of the slice: x: 4, y: 4, z: 8, core: 2. Of those that a mesh axis runs over, the one named last changes fastest.
Arguments:
- affinity_tiles: bfloat16 [1024, 64, 128, 128], P(('row', 'col'))
- block_columns: int32 [1024, 64], P(('row', 'col')), may hold values from 0 to 127, as said below
- live_counts: int32 [8, 128], P('row', 'col'), may hold values from 1 to 64, 4096 in all within a row
- earlier_blocks: float32 [4, 64, 131072], P(None, None, ('row', 'col')), may hold values from -6 to 6
Outputs:
- new_blocks: float32 [2, 64, 131072], P(None, None, ('row', 'col'))
- triangular_factors: float32 [2, 64, 64], replicated
Inputs may be any that keep to these rules, and one draw needn't show every extreme that they name: `block_columns`: slot 0 of every block row names the block row itself; columns name block rows of the same row group. `live_counts`: slots at or past a block row's count are ignored.
All inputs are finite; a program needn't handle non-finite values.
Results may differ from a plain program's by a relative error of at most 0.0059.
Values may be sent and summed in bfloat16 or wider, within the bound.
No kernel may reach another device: no remote copies, remote signals or barrier semaphores. Data moves between devices by JAX's collectives and lax.ppermute only.
A program may use at most 64 MiB of HBM per device.

v0:
```python
import jax
import jax.numpy as jnp
from jax import lax
from jax.sharding import PartitionSpec as P

STEPS = 2


def apply_tiles(affinity_tiles, block_columns, row_counts, group_blocks):
    block_rows = affinity_tiles.shape[0]
    slot_count = affinity_tiles.shape[1]
    tile_size = affinity_tiles.shape[2]
    block_width = group_blocks.shape[0]
    slot_ids = lax.broadcasted_iota(jnp.int32, (block_rows, slot_count), 1)
    live_mask = slot_ids < row_counts[:, None]
    picked = jnp.take(group_blocks, block_columns, axis=1)
    picked = jnp.where(live_mask[None, :, :, None], picked, jnp.zeros((), jnp.bfloat16))
    running = jnp.einsum(
        "rsij,brsj->bri", affinity_tiles, picked, preferred_element_type=jnp.float32
    )
    return running.reshape(block_width, block_rows * tile_size)


def on_device(affinity_tiles, block_columns, live_counts, earlier_blocks):
    block_rows = affinity_tiles.shape[0]
    tile_size = affinity_tiles.shape[2]
    block_width = earlier_blocks.shape[1]
    rows_here = earlier_blocks.shape[2]
    total_rows = rows_here * lax.axis_size("row") * lax.axis_size("col")
    row_counts = live_counts.reshape(block_rows)
    known_list = [earlier_blocks[i] for i in range(earlier_blocks.shape[0])]
    first_half = known_list[-1].astype(jnp.bfloat16)
    group_half = lax.all_gather(first_half, "col", axis=1, tiled=True)
    fresh_list = []
    factor_list = []
    for step_index in range(STEPS):
        is_last = step_index + 1 == STEPS
        group_blocks = group_half.reshape(block_width, -1, tile_size)
        product = apply_tiles(affinity_tiles, block_columns, row_counts, group_blocks)
        known = jnp.concatenate(known_list, 0)
        local_proj = jnp.dot(known, product.T, precision=lax.Precision.HIGHEST) / total_rows
        projections = lax.psum(local_proj, ("row", "col"))
        residual = product - jnp.dot(projections.T, known, precision=lax.Precision.HIGHEST)
        local_gram = jnp.dot(residual, residual.T, precision=lax.Precision.HIGHEST) / total_rows
        gram_sum = lax.psum(local_gram, ("row", "col"))
        factor_low = jnp.linalg.cholesky(gram_sum)
        fresh = jax.scipy.linalg.solve_triangular(factor_low, residual, lower=True)
        fresh_list.append(fresh)
        factor_list.append(factor_low.T)
        known_list.append(fresh)
        if not is_last:
            group_half = lax.all_gather(fresh.astype(jnp.bfloat16), "col", axis=1, tiled=True)
    return (jnp.stack(fresh_list), jnp.stack(factor_list))


def solution(mesh):
    return jax.shard_map(
        on_device,
        mesh=mesh,
        in_specs=(
            P(("row", "col"), None, None, None),
            P(("row", "col"), None),
            P("row", "col"),
            P(None, None, ("row", "col")),
        ),
        out_specs=(P(None, None, ("row", "col")), P()),
        check_vma=False,
    )
```

profile of v0, /device:TPU:1, one launch (start us, length us, event | category | flops | bytes accessed | tf_op | source)
XLA Modules:
  0.0 864.7 jit_solution(17645085274301516106)
XLA Ops:
  7.2 1.5 fusion.32
  8.8 0.7 compare_select_fusion
  9.6 0.8 iota_compare_fusion.2
  10.4 0.9 constant_dynamic-update-slice_fusion.4
  11.3 0.9 constant_dynamic-update-slice_fusion.3
  12.2 0.9 constant_dynamic-update-slice_fusion.2
  13.1 1.1 slice_bitcast_fusion.2
  14.3 71.6 %all-gather.3.cloned.1.call-done = bf16[64,16384]{1,0:T(8,128)(2,1)} async-done(((bf16[64,512]{1,0:T(8,128)(2,1)}), bf16[64,16384]{1,0:T(8,128)(2,1)}) %all-gather.3.cloned.1.call-update) | async-done | bytes 2097168 | tf_op jit(solution)/shard_map/all_gather | solution.py:33
  85.9 2.2 copy_bitcast_fusion.1
  88.1 3.0 gather_fusion
  91.1 6.3 fusion.12
  97.3 1.2 convolution_multiply_fusion.1
  98.6 0.9 constant_dynamic-update-slice_fusion.1
  99.6 246.5 %all-reduce.3.cloned.1.call-done = f32[256,64]{1,0:T(8,128)} async-done(((f32[256,64]{1,0:T(8,128)}), f32[256,64]{1,0:T(8,128)}) %all-reduce.3.cloned.1.call-update) | async-done | bytes 65552 | tf_op jit(solution)/shard_map/psum | solution.py:42
  346.0 1.3 convolution_subtract_fusion.1
  347.6 76.2 %psum.29 = f32[64,64]{0,1:T(8,128)S(1)} all-reduce(f32[64,64]{0,1:T(8,128)S(1)} %convolution_multiply_fusion.3), channel_id=1, replica_groups=mesh['row'=8,'col'=32] {'row','col'}, use_global_device_ids=true, to_apply=%region_1.3 | all-reduce | flops 4096 | bytes 32768 | tf_op jit(solution)/shard_map/psum | solution.py:45
  423.9 5.8 cholesky.44
  430.4 0.7 fusion.24
  431.1 4.9 custom-call.6
  436.0 1.0 fusion.33
  437.0 66.8 %all-gather.5.cloned.1.call-done = bf16[64,16384]{1,0:T(8,128)(2,1)} async-done(((bf16[64,512]{1,0:T(8,128)(2,1)}), bf16[64,16384]{1,0:T(8,128)(2,1)}) %all-gather.5.cloned.1.call-update) | async-done | bytes 2097168 | tf_op jit(solution)/shard_map/all_gather | solution.py:52
  503.8 2.2 copy_bitcast_fusion
  506.0 3.0 gather_fusion.1
  509.0 6.3 fusion.13
  515.3 1.3 convolution_multiply_fusion
  516.7 251.0 %all-reduce.5.cloned.1.call-done = f32[320,64]{1,0:T(8,128)} async-done(((f32[320,64]{1,0:T(8,128)}), f32[320,64]{1,0:T(8,128)}) %all-reduce.5.cloned.1.call-update) | async-done | bytes 81936 | tf_op jit(solution)/shard_map/psum | solution.py:42
  767.7 1.5 convolution_subtract_fusion
  769.4 74.8 %psum.31 = f32[64,64]{0,1:T(8,128)S(1)} all-reduce(f32[64,64]{0,1:T(8,128)S(1)} %convolution_multiply_fusion.2), channel_id=1, replica_groups=mesh['row'=8,'col'=32] {'row','col'}, use_global_device_ids=true, to_apply=%region_5.9 | all-reduce | flops 4096 | bytes 32768 | tf_op jit(solution)/shard_map/psum | solution.py:45
  844.3 5.8 cholesky.55
  851.5 0.7 copy.21
  852.2 4.9 custom-call.7
  857.4 0.7 pad_maximum_fusion.3
  (23 shorter events, 3.3 us)
Async XLA Ops:
  7.2 78.7 %all-gather.3.cloned.1.call-start = ((), (), s32[]{:S(2)}) async-start(), calls=%async_computation | async-start | bytes 2162688 | tf_op jit(solution)/shard_map/all_gather | solution.py:33
  8.8 337.2 %all-reduce.3.cloned.1.call-start = ((), (), s32[]{:S(2)}) async-start(), calls=%async_computation.1 | async-start | bytes 262144 | tf_op jit(solution)/shard_map/psum | solution.py:42
  98.6 405.2 %all-gather.5.cloned.1.call-start = ((), (), s32[]{:S(2)}) async-start(), calls=%async_computation.2 | async-start | bytes 2162688 | tf_op jit(solution)/shard_map/all_gather | solution.py:52
  437.0 330.7 %all-reduce.5.cloned.1.call-start = ((), (), s32[]{:S(2)}) async-start(), calls=%async_computation.3 | async-start | bytes 327680 | tf_op jit(solution)/shard_map/psum | solution.py:42
Sparse Core Ops, SparseCore 0:
  11.0 74.8 all-gather.2
  98.7 247.2 all-reduce.2
  437.1 66.6 all-gather.4
  516.8 250.8 all-reduce.4
where the time goes:
time: 865 us
  waiting for transfers between devices  636 us (74%)
  blocking collectives  151 us (17%)
  other arithmetic  26.4 us (3%)
  matrix products  19.7 us (2%)
  local copies, waits for them, and re-layouts  17.7 us (2%)
  between operations  13.9 us (2%)
    psum x2, waiting for transfers between devices, on_device(): projections = lax.psum(local_proj, ('row', 'col'))  497 us
    psum x2, blocking collectives, on_device(): gram_sum = lax.psum(local_gram, ('row', 'col'))  151 us
    all_gather x1, waiting for transfers between devices, on_device(): group_half = lax.all_gather(first_half, 'col', axis=1, tiled=True)  71.6 us
    all_gather x1, waiting for transfers between devices, on_device(): lax.all_gather(fresh.astype(jnp.bfloat16), 'col', axis=1, tiled=True)  66.8 us
  transfers between devices with their start and end apart: 4, of which 4 were waited for; matrix products, arithmetic and copies ran while one was open for 1% of the time, Pallas kernels for 0%

commit v1 on v0

--- a/solution.py
+++ b/solution.py
@@ -39,7 +39,8 @@
         product = apply_tiles(affinity_tiles, block_columns, row_counts, group_blocks)
         known = jnp.concatenate(known_list, 0)
         local_proj = jnp.dot(known, product.T, precision=lax.Precision.HIGHEST) / total_rows
-        projections = lax.psum(local_proj, ("row", "col"))
+        parts = lax.all_gather(local_proj, ("row", "col"))
+        projections = jnp.sum(parts, axis=0)
         residual = product - jnp.dot(projections.T, known, precision=lax.Precision.HIGHEST)
         local_gram = jnp.dot(residual, residual.T, precision=lax.Precision.HIGHEST) / total_rows
         gram_sum = lax.psum(local_gram, ("row", "col"))

time: 865 us -> 672 us (0.78)
  waiting for transfers between devices: 636 us -> 413 us
  other arithmetic: 26.4 us -> 43.3 us
  local copies, waits for them, and re-layouts: 17.7 us -> 29.9 us
    psum x2 -> x0, waiting for transfers between devices: 497 us -> none  [on_device(): projections = lax.psum(local_proj, ('row', 'col'))]
    all_gather x0 -> x2, waiting for transfers between devices: none -> 272 us  [on_device(): parts = lax.all_gather(local_proj, ('row', 'col'))]
    reduce_sum x0 -> x2, other arithmetic: none -> 17 us  [on_device(): projections = jnp.sum(parts, axis=0)]
    unnamed x5 -> x8, local copies, waits for them, and re-layouts: 4.38 us -> 16.6 us
  transfers between devices with their start and end apart: 4 -> 4, of which waited for: 4 -> 4; matrix products, arithmetic and copies ran while one was open for 1% -> 0% of each run, Pallas kernels for 0% -> 0%
where the time goes in v1:
time: 672 us; the launch traced here: 671 us
  waiting for transfers between devices  413 us (61%)
  blocking collectives  153 us (23%)
  other arithmetic  43.3 us (6%)
  local copies, waits for them, and re-layouts  29.9 us (4%)
  matrix products  18 us (3%)
  between operations  13.9 us (2%)
    all_gather x2, waiting for transfers between devices, on_device(): parts = lax.all_gather(local_proj, ('row', 'col'))  272 us
    psum x2, blocking collectives, on_device(): gram_sum = lax.psum(local_gram, ('row', 'col'))  153 us
    all_gather x1, waiting for transfers between devices, on_device(): group_half = lax.all_gather(first_half, 'col', axis=1, tiled=True)  74.4 us
    all_gather x1, waiting for transfers between devices, on_device(): lax.all_gather(fresh.astype(jnp.bfloat16), 'col', axis=1, tiled=True)  66.3 us
    reduce_sum x2, other arithmetic, on_device(): projections = jnp.sum(parts, axis=0)  17 us
    unnamed x8, local copies, waits for them, and re-layouts  16.6 us
  transfers between devices with their start and end apart: 4, of which 4 were waited for; matrix products, arithmetic and copies ran while one was open for 0% of the time, Pallas kernels for 0%

profile of v1, /device:TPU:1, one launch (start us, length us, event | category | flops | bytes accessed | tf_op | source)
XLA Modules:
  0.0 671.3 jit_solution(1902080720864810698)
XLA Ops:
  7.2 1.5 fusion.33
  8.8 0.7 compare_select_fusion
  9.6 0.8 iota_compare_fusion.2
  10.4 1.1 slice_bitcast_fusion.2
  11.5 74.4 %all-gather.8.cloned.1.call-done = bf16[64,16384]{1,0:T(8,128)(2,1)} async-done(((bf16[64,512]{1,0:T(8,128)(2,1)}), bf16[64,16384]{1,0:T(8,128)(2,1)}) %all-gather.8.cloned.1.call-update) | async-done | bytes 2097168 | tf_op jit(solution)/shard_map/all_gather | solution.py:33
  85.9 2.2 copy_bitcast_fusion.1
  88.1 3.0 gather_fusion
  91.1 6.3 fusion.12
  97.4 1.2 convolution_multiply_fusion.1
  98.8 131.4 %all-gather.12.cloned.1.call-done = f32[65536,64]{0,1:T(8,128)} async-done(((f32[256,64]{0,1:T(8,128)}), f32[65536,64]{0,1:T(8,128)}) %all-gather.12.cloned.1.call-update) | async-done | bytes 16777232 | tf_op jit(solution)/shard_map/all_gather | solution.py:42
  230.2 15.8 %copy.39 = f32[8,8,256,256]{3,2,1,0:T(8,128)} copy(f32[8,8,256,256]{3,1,2,0:T(8,128)} %bitcast.111) | data formatting | bytes 33554432
  246.1 7.5 %bitcast_reduce_fusion = f32[256,64]{0,1:T(8,128)S(1)} fusion(f32[8,8,256,256]{3,2,1,0:T(8,128)} %copy.39), kind=kLoop, calls=%fused_computation.2 | loop fusion | flops 4177920 | bytes 16842752 | tf_op jit(solution)/shard_map/reduce_sum | solution.py:43
  254.3 78.2 %psum.14 = f32[64,64]{0,1:T(8,128)S(1)} all-reduce(f32[64,64]{0,1:T(8,128)S(1)} %convolution_multiply_fusion.3), channel_id=1, replica_groups=mesh['row'=8,'col'=32] {'row','col'}, use_global_device_ids=true, to_apply=%region_1.3 | all-reduce | flops 4096 | bytes 32768 | tf_op jit(solution)/shard_map/psum | solution.py:46
  332.5 5.8 cholesky.44
  338.4 0.6 compare_reduce_fusion.1
  339.1 0.7 fusion.25
  339.7 4.9 custom-call.6
  344.6 1.0 fusion.34
  345.9 66.3 %all-gather.10.cloned.1.call-done = bf16[64,16384]{1,0:T(8,128)(2,1)} async-done(((bf16[64,512]{1,0:T(8,128)(2,1)}), bf16[64,16384]{1,0:T(8,128)(2,1)}) %all-gather.10.cloned.1.call-update) | async-done | bytes 2097168 | tf_op jit(solution)/shard_map/all_gather | solution.py:53
  412.1 2.2 copy_bitcast_fusion
  414.3 3.0 gather_fusion.1
  417.3 6.3 fusion.13
  423.6 1.4 fusion.14
  425.0 140.9 %all-gather.14.cloned.1.call-done = f32[256,320,64]{1,2,0:T(8,128)} async-done(((f32[1,320,64]{1,2,0:T(8,128)}), f32[256,320,64]{1,2,0:T(8,128)}) %all-gather.14.cloned.1.call-update) | async-done | bytes 20971536 | tf_op jit(solution)/shard_map/all_gather | solution.py:42
  565.8 9.5 %reduce_sum.19 = f32[320,64]{0,1:T(8,128)S(1)} reduce(f32[256,320,64]{1,2,0:T(8,128)} %all-gather.14.cloned.1.call-done, f32[]{:T(128)} %constant.52.clone.1), dimensions={0}, to_apply=%region_4.8 | reduce | flops 5222400 | bytes 21053444 | tf_op jit(solution)/shard_map/reduce_sum | solution.py:43
  576.1 74.7 %psum.15 = f32[64,64]{0,1:T(8,128)S(1)} all-reduce(f32[64,64]{0,1:T(8,128)S(1)} %convolution_multiply_fusion.2), channel_id=1, replica_groups=mesh['row'=8,'col'=32] {'row','col'}, use_global_device_ids=true, to_apply=%region_5.9 | all-reduce | flops 4096 | bytes 32768 | tf_op jit(solution)/shard_map/psum | solution.py:46
  650.9 5.8 cholesky.55
  656.8 0.6 compare_reduce_fusion
  657.5 0.7 fusion.26
  658.1 0.7 copy.30
  658.8 4.9 custom-call.7
  664.1 0.7 pad_maximum_fusion.3
  (28 shorter events, 2.6 us)
Async XLA Ops:
  7.2 78.7 %all-gather.8.cloned.1.call-start = ((), (), s32[]{:S(2)}) async-start(), calls=%async_computation | async-start | bytes 2162688 | tf_op jit(solution)/shard_map/all_gather | solution.py:33
  8.8 221.5 %all-gather.12.cloned.1.call-start = ((), (), s32[]{:S(2)}) async-start(), calls=%async_computation.2 | async-start | bytes 16842752 | tf_op jit(solution)/shard_map/all_gather | solution.py:42
  91.1 7.6 %copy-start = (f32[4,64,512]{2,1,0:T(8,128)S(1)}, f32[4,64,512]{2,1,0:T(8,128)}, u32[]{:S(2)}) copy-start(f32[4,64,512]{2,1,0:T(8,128)} %param.12) | copy-start | bytes 1572868
  98.7 313.4 %all-gather.10.cloned.1.call-start = ((), (), s32[]{:S(2)}) async-start(), calls=%async_computation.1 | async-start | bytes 2162688 | tf_op jit(solution)/shard_map/all_gather | solution.py:53
  345.6 220.2 %all-gather.14.cloned.1.call-start = ((), (), s32[]{:S(2)}) async-start(), calls=%async_computation.3 | async-start | bytes 25264128 | tf_op jit(solution)/shard_map/all_gather | solution.py:42
Sparse Core Ops, SparseCore 0:
  11.0 74.8 all-gather.7
  98.8 131.4 all-gather.11
  345.7 66.3 all-gather.9
  425.1 140.7 all-gather.13
